TPU v7x, 128 devices: a whole 4x4x4 slice. The times are simulated.
128 devices in a mesh: section: 4 (over x), tensor: 32 (over y, z, core).
Axes of the slice: x: 4, y: 4, z: 4, core: 2. Of those that a mesh axis runs over, the one named last changes fastest.
Arguments:
- hidden_last: bfloat16 [512, 6656], P(None, 'tensor'), may hold values from -6 to 6
- labels: int32 [512], replicated, may hold values from 0 to 31999
- head_weight: bfloat16 [6656, 32000], P(None, 'tensor'), may hold values from -0.21875 to 0.21875
- layer_inputs: bfloat16 [4, 512, 6656], P('section', None, 'tensor'), may hold values from -6 to 6
- weights: bfloat16 [4, 6656, 6656], P('section', 'tensor'), may hold values from -0.078125 to 0.078125
- row_state: float32 [4, 6656], P('section', 'tensor'), may hold values from 1.173753e-06 to 0.000498845
- col_state: float32 [4, 6656], P('section'), may hold values from 1e-08 to 1e-06
Outputs:
- loss: float32 [], replicated
- input_grads: bfloat16 [4, 512, 6656], P('section', None, 'tensor')
- new_weights: bfloat16 [4, 6656, 6656], P('section', 'tensor')
- new_row_state: float32 [4, 6656], P('section', 'tensor')
- new_col_state: float32 [4, 6656], P('section')
All inputs are finite; a program needn't handle non-finite values.
Results may differ from a plain program's by a relative error of at most 0.007.
Values may be sent and summed in bfloat16 or wider, within the bound.
No kernel may reach another device: no remote copies, remote signals or barrier semaphores. Data moves between devices by JAX's collectives and lax.ppermute only.
A program may use at most 128 MiB of HBM per device.

v0:
```python
import jax
import jax.numpy as jnp
from jax import lax
from jax.sharding import PartitionSpec as P

decay_rate = 0.9
learn_rate = 0.3
tiny_term = 1e-30


def copy_for_each(x, axis):
    peers = lax.axis_size(axis)
    return lax.all_to_all(jnp.broadcast_to(x[None], (peers, *x.shape)), axis, 0, 0, tiled=True)


def taken_together(x, axis):
    return copy_for_each(x, axis).sum(axis=0)


def in_one(arrays, axis):
    ravelled, at, done = (jnp.concatenate([a.reshape(-1) for a in arrays]), 0, [])
    subtotal = taken_together(ravelled, axis)
    for a in arrays:
        done.append(subtotal[at : at + a.size].reshape(a.shape))
        at += a.size
    return tuple(done)


def joined_along(blocks, dim):
    lengths = list(blocks.shape[1:])
    lengths[dim] *= blocks.shape[0]
    return jnp.moveaxis(blocks, 0, dim).reshape(lengths)


def collect(x, axis, dim):
    return joined_along(copy_for_each(x, axis), dim)


def shifted(block, axis, distance):
    devices = range(lax.axis_size(axis))
    route = [(i - distance, i) for i in devices if i - distance in devices]
    return lax.ppermute(block, axis, route)


def body(hidden_last, labels, head_weight, layer_inputs, weights, row_state, col_state):
    section_count = lax.axis_size("section")
    section_index = lax.axis_index("section")
    all_rows = labels.shape[0]
    model_width = head_weight.shape[0]
    vocab_local = head_weight.shape[1]
    local_weight = weights[0]
    rows_local = local_weight.shape[0]
    saved_all = layer_inputs[0]
    columns = lax.axis_index("tensor") * vocab_local + lax.iota(jnp.int32, vocab_local)
    share_rows = all_rows // section_count
    row_start = section_index * share_rows
    hidden_rows = lax.dynamic_slice_in_dim(hidden_last, row_start, share_rows, 0)
    head_slice = head_weight
    logits = jnp.dot(
        lax.all_gather(hidden_rows, "tensor", axis=1, tiled=True),
        head_slice,
        preferred_element_type=jnp.float32,
    )
    exponent = jnp.exp(logits)
    label_hit = (
        lax.dynamic_slice_in_dim(labels, row_start, share_rows, 0)[:, None] == columns[None, :]
    )
    denominator, picked = in_one(
        (
            jnp.sum(exponent, axis=1),
            jnp.sum(jnp.where(label_hit, logits, jnp.zeros_like(logits)), axis=1),
        ),
        "tensor",
    )
    losses = jnp.log(denominator) - picked
    logit_grad = (
        (exponent / denominator[:, None] - label_hit.astype(jnp.float32)) / all_rows
    ).astype(jnp.bfloat16)
    head_slice = head_weight
    shares = lax.psum_scatter(
        lax.dot_general(
            head_slice, logit_grad, (((1,), (1,)), ((), ())), preferred_element_type=jnp.float32
        ),
        "tensor",
        scatter_dimension=0,
        tiled=True,
    )
    part_grad = shares.T.astype(jnp.bfloat16)
    part_loss = jnp.sum(losses)
    head_grad = collect(part_grad, "section", 0)
    loss = lax.psum(part_loss, "section") / all_rows
    is_last = section_index == section_count - 1

    def layer_block(dy_rows, saved_rows):
        gathered = lax.all_gather(dy_rows, "tensor", axis=1, tiled=True)
        backward = lax.dot_general(
            gathered, local_weight, (((1,), (1,)), ((), ())), preferred_element_type=jnp.float32
        )
        product = lax.dot_general(
            saved_rows, gathered, (((0,), (0,)), ((), ())), preferred_element_type=jnp.float32
        )
        backward, piece_grad = (backward, product)
        input_grad = (dy_rows.astype(jnp.float32) + backward).astype(jnp.bfloat16)
        return (input_grad, piece_grad)

    start_grad = jnp.zeros((rows_local, model_width), jnp.float32)

    def advance_whole(step_index, loop_state):
        received, gradient, outputs = loop_state
        active = step_index == section_count - 1 - section_index
        dy_rows = jnp.where(is_last, head_grad, received)
        input_grad, piece_grad = layer_block(dy_rows, saved_all)
        gradient = gradient + jnp.where(active, piece_grad, jnp.zeros_like(piece_grad))
        outputs = jnp.where(active, input_grad, outputs)
        received = shifted(input_grad, "section", -1)
        return (received, gradient, outputs)

    loop_state = (
        jnp.zeros((all_rows, rows_local), jnp.bfloat16),
        start_grad,
        jnp.zeros((all_rows, rows_local), jnp.bfloat16),
    )
    loop_state = lax.fori_loop(0, section_count, advance_whole, loop_state)
    gradient = loop_state[1]
    outputs = loop_state[2]
    weight_float = local_weight.astype(jnp.float32)
    squares = gradient * gradient + tiny_term
    row_new = decay_rate * row_state[0] + (1.0 - decay_rate) * jnp.mean(squares, axis=1)
    col_part = jnp.sum(squares, axis=0)
    entries = float(model_width * model_width)
    col_sum, row_total, weight_total = in_one(
        (col_part, jnp.sum(row_new), jnp.sum(weight_float * weight_float)), "tensor"
    )
    col_new = decay_rate * col_state[0] + (1.0 - decay_rate) * (col_sum / model_width)
    update = gradient / jnp.sqrt(row_new[:, None] * col_new[None, :] / row_total)
    update_total = taken_together(jnp.sum(update * update), "tensor")
    factor = (
        learn_rate
        * jnp.sqrt(weight_total / entries)
        / jnp.maximum(1.0, jnp.sqrt(update_total / entries))
    )
    new_weight = (weight_float - factor * update).astype(jnp.bfloat16)
    return (loss, outputs[None], new_weight[None], row_new[None], col_new[None])


def solution(mesh):
    return jax.shard_map(
        body,
        mesh=mesh,
        in_specs=(
            P(None, "tensor"),
            P(),
            P(None, "tensor"),
            P("section", None, "tensor"),
            P("section", "tensor", None),
            P("section", "tensor"),
            P("section", None),
        ),
        out_specs=(
            P(),
            P("section", None, "tensor"),
            P("section", "tensor", None),
            P("section", "tensor"),
            P("section", None),
        ),
        check_vma=False,
    )
```

profile of v0, /device:TPU:0, one launch (start us, length us, event | category | flops | bytes accessed | tf_op | source)
XLA Modules:
  0.0 518.1 jit_solution(7403697374861706777)
XLA Ops:
  7.2 0.9 copy-done
  8.1 0.6 constant_dynamic-slice_fusion
  8.8 0.8 dynamic_slice.7
  9.6 47.4 %all-gather.3.cloned.1.call-done = bf16[128,6656]{0,1:T(8,128)(2,1)} async-done(((bf16[128,208]{0,1:T(8,128)(2,1)}), bf16[128,6656]{0,1:T(8,128)(2,1)}) %all-gather.3.cloned.1.call-update) | async-done | bytes 1703952 | tf_op jit(solution)/shard_map/all_gather | solution.py:60
  57.0 7.4 %exponential_reduce_fusion = (f32[128]{0:T(128)S(1)}, f32[128]{0:T(128)S(1)}, f32[128,1000]{0,1:T(8,128)S(1)}) fusion(s32[1000]{0:T(1024)S(1)} %iota_add_fusion, s32[128]{0:T(128)S(1)} %dynamic_slice.7, bf16[128,6656]{0,1:T(8,128)(2,1)} %all-gather.3.cloned.1.call-done, bf16[6656,1000]{0,1:T(8,128)(2,1)} %param.11), kind=kOutput, calls=%fused_computation.24 | convolution fusion | flops 1704447744 | bytes 15533472 | tf_op jit(solution)/shard_map/dot_general | solution.py:59
  64.4 12.4 %all_to_all.23 = f32[32,1,256]{2,1,0:T(1,128)S(1)} all-to-all(f32[32,1,256]{2,1,0:T(1,128)S(1)} %broadcast_in_dim.17), channel_id=1, replica_groups=mesh['section'=4,'tensor'=32] {'tensor'}, dimensions={0} | all-to-all | bytes 65536 | tf_op jit(solution)/shard_map/all_to_all | solution.py:13
  76.9 0.6 fusion.24
  77.5 8.7 %convolution_bitcast_fusion = f32[6656,128]{0,1:T(8,128)} fusion(bf16[6656,1000]{0,1:T(8,128)(2,1)} %param.11, f32[128,1000]{0,1:T(8,128)S(1)} %get-tuple-element.282, f32[128]{0:T(128)S(1)} %get-tuple-element.280, s32[128]{0:T(128)S(1)} %dynamic_slice.7, s32[1000]{0:T(1024)S(1)} %iota_add_fusion), kind=kOutput, calls=%fused_computation.7 | convolution fusion | flops 1704704000 | bytes 17236896 | tf_op jit(solution)/shard_map/dot_general | solution.py:81
  86.2 5.1 copy.28
  91.4 0.1 copy.25
  91.5 78.6 %reduce-scatter.4.cloned.1.call-done = f32[208,128]{1,0:T(8,128)} async-done(((f32[6656,128]{1,0:T(8,128)}), f32[208,128]{1,0:T(8,128)}) %reduce-scatter.4.cloned.1.call-update) | async-done | bytes 106512
  170.1 1.0 copy.29
  171.2 0.7 broadcast_in_dim.18
  171.9 4.3 all-to-all-start.1
  176.2 2.0 fusion.3
  178.2 4.5 all-to-all-done.1
  182.7 0.9 copy_bitcast_fusion
  183.6 0.7 broadcast.62
  184.3 270.2 %while.20 = (s32[]{:T(128)}, bf16[512,208]{0,1:T(8,128)(2,1)}, f32[208,6656]{1,0:T(8,128)}, bf16[512,208]{0,1:T(8,128)(2,1)}, pred[]{:T(512)}, /*index=5*/bf16[5...) while((s32[]{:T(128)}, bf16[512,208]{0,1:T(8,128)(2,1)}, ...), condition=%wide.region_7.8_spmd.clone, body=%wide.region_6.7_spmd.clone.sunk | while | flops 2840141824 | bytes 111182184 | solution.py:123
  184.4 1.6 broadcast_select_fusion.2
  186.0 49.6 %all-gather.5.cloned.1.call-done = bf16[512,6656]{0,1:T(8,128)(2,1)} async-done(((bf16[512,208]{0,1:T(8,128)(2,1)}), bf16[512,6656]{0,1:T(8,128)(2,1)}) %all-gather.5.cloned.1.call-update) | async-done | bytes 6815760 | tf_op jit(solution)/shard_map/while/body/eval_jaxpr/all_gather | solution.py:95
  235.6 5.4 %select_select_fusion.2 = (bf16[512,208]{0,1:T(8,128)(2,1)}, bf16[512,208]{0,1:T(8,128)(2,1)S(1)}) fusion(bf16[512,208]{0,1:T(8,128)(2,1)} %get-tuple-element.356, pred[]{:T(512)S(6)} %compare.3, pred[]{:T(512)S(6)} %eq.52, bf16[208,6656]{1,0:T(8,128)(2,1)S(1)} %get-tuple-element.370, bf16[512,6656]{0,1:T(8,128)(2,1)} %all-gather.5.cloned.1.call-done, ...), kind=kOutput, calls=%fused_computation.5.clone.1 | convolution fusion | flops 1418207232 | bytes 10436610 | tf_op jit(solution)/shard_map/while/body/eval_jaxpr/dot_general | solution.py:96
  241.0 1.4 collective-permute-start
  242.5 3.5 fusion.42
  246.0 4.5 collective-permute-done
  250.4 0.7 copy-done.3
  251.1 1.6 broadcast_select_fusion.2
  252.8 50.7 %all-gather.5.cloned.1.call-done = bf16[512,6656]{0,1:T(8,128)(2,1)} async-done(((bf16[512,208]{0,1:T(8,128)(2,1)}), bf16[512,6656]{0,1:T(8,128)(2,1)}) %all-gather.5.cloned.1.call-update) | async-done | bytes 6815760 | tf_op jit(solution)/shard_map/while/body/eval_jaxpr/all_gather | solution.py:95
  303.4 5.4 %select_select_fusion.2 = (bf16[512,208]{0,1:T(8,128)(2,1)}, bf16[512,208]{0,1:T(8,128)(2,1)S(1)}) fusion(bf16[512,208]{0,1:T(8,128)(2,1)} %get-tuple-element.356, pred[]{:T(512)S(6)} %compare.3, pred[]{:T(512)S(6)} %eq.52, bf16[208,6656]{1,0:T(8,128)(2,1)S(1)} %get-tuple-element.370, bf16[512,6656]{0,1:T(8,128)(2,1)} %all-gather.5.cloned.1.call-done, ...), kind=kOutput, calls=%fused_computation.5.clone.1 | convolution fusion | flops 1418207232 | bytes 10436610 | tf_op jit(solution)/shard_map/while/body/eval_jaxpr/dot_general | solution.py:96
  308.8 1.4 collective-permute-start
  310.3 3.5 fusion.42
  313.8 4.5 collective-permute-done
  318.2 0.7 copy-done.3
  318.9 1.6 broadcast_select_fusion.2
  320.6 50.7 %all-gather.5.cloned.1.call-done = bf16[512,6656]{0,1:T(8,128)(2,1)} async-done(((bf16[512,208]{0,1:T(8,128)(2,1)}), bf16[512,6656]{0,1:T(8,128)(2,1)}) %all-gather.5.cloned.1.call-update) | async-done | bytes 6815760 | tf_op jit(solution)/shard_map/while/body/eval_jaxpr/all_gather | solution.py:95
  371.3 5.4 %select_select_fusion.2 = (bf16[512,208]{0,1:T(8,128)(2,1)}, bf16[512,208]{0,1:T(8,128)(2,1)S(1)}) fusion(bf16[512,208]{0,1:T(8,128)(2,1)} %get-tuple-element.356, pred[]{:T(512)S(6)} %compare.3, pred[]{:T(512)S(6)} %eq.52, bf16[208,6656]{1,0:T(8,128)(2,1)S(1)} %get-tuple-element.370, bf16[512,6656]{0,1:T(8,128)(2,1)} %all-gather.5.cloned.1.call-done, ...), kind=kOutput, calls=%fused_computation.5.clone.1 | convolution fusion | flops 1418207232 | bytes 10436610 | tf_op jit(solution)/shard_map/while/body/eval_jaxpr/dot_general | solution.py:96
  376.7 1.4 collective-permute-start
  378.1 3.5 fusion.42
  381.6 4.5 collective-permute-done
  386.1 0.7 copy-done.3
  386.8 1.6 broadcast_select_fusion.2
  388.4 50.7 %all-gather.5.cloned.1.call-done = bf16[512,6656]{0,1:T(8,128)(2,1)} async-done(((bf16[512,208]{0,1:T(8,128)(2,1)}), bf16[512,6656]{0,1:T(8,128)(2,1)}) %all-gather.5.cloned.1.call-update) | async-done | bytes 6815760 | tf_op jit(solution)/shard_map/while/body/eval_jaxpr/all_gather | solution.py:95
  439.1 5.4 %select_select_fusion.2 = (bf16[512,208]{0,1:T(8,128)(2,1)}, bf16[512,208]{0,1:T(8,128)(2,1)S(1)}) fusion(bf16[512,208]{0,1:T(8,128)(2,1)} %get-tuple-element.356, pred[]{:T(512)S(6)} %compare.3, pred[]{:T(512)S(6)} %eq.52, bf16[208,6656]{1,0:T(8,128)(2,1)S(1)} %get-tuple-element.370, bf16[512,6656]{0,1:T(8,128)(2,1)} %all-gather.5.cloned.1.call-done, ...), kind=kOutput, calls=%fused_computation.5.clone.1 | convolution fusion | flops 1418207232 | bytes 10436610 | tf_op jit(solution)/shard_map/while/body/eval_jaxpr/dot_general | solution.py:96
  444.5 1.4 collective-permute-start
  446.0 3.5 fusion.42
  449.5 4.5 collective-permute-done
  453.9 0.7 copy-done.3
  454.6 4.5 fusion.5
  459.1 0.6 fusion.20
  459.7 0.6 fusion.21
  460.3 1.3 concatenate.7
  461.6 1.4 broadcast_in_dim.20
  463.0 4.9 all-to-all-start.2
  468.0 9.9 %psum.7 = f32[]{:T(128)} all-reduce(f32[]{:T(128)} %get-tuple-element.281), channel_id=1, replica_groups=mesh['section'=4,'tensor'=32] {'section'}, use_global_device_ids=true, to_apply=%region_4.5 | all-reduce | flops 1 | bytes 8 | tf_op jit(solution)/shard_map/psum | solution.py:91
  478.5 4.1 all-to-all-done.2
  482.6 1.7 reduce_sum.107
  484.3 0.6 fusion.23
  484.9 0.6 broadcast_in_dim.23
  485.5 5.4 %multiply_reduce_fusion = f32[]{:T(128)} fusion(f32[208,6656]{1,0:T(8,128)} %get-tuple-element.219, f32[]{:T(128)} %bitcast.9, f32[6656]{0:T(1024)S(1)} %fusion.17, f32[208]{0:T(256)S(1)} %get-tuple-element.273), kind=kLoop, calls=%fused_computation.12 | loop fusion | flops 6922239 | bytes 5565256 | tf_op jit(solution)/shard_map/reduce_sum | solution.py:136
  490.9 1.2 broadcast_in_dim.21
  492.2 4.2 all-to-all-start.3
  496.9 6.7 %all-to-all-done.3 = f32[32,1,1]{2,1,0:T(1,128)S(1)} async-done(((f32[32,1,1]{2,1,0:T(1,128)}), f32[32,1,1]{2,1,0:T(1,128)S(1)}, u32[]{:S(2)}, u32[]{:S(2)}) %all-to-all-start.3) | async-done | bytes 160 | tf_op jit(solution)/shard_map/all_to_all | solution.py:13
  503.6 0.6 reduce_sum.109
  505.0 5.2 fusion.7
  (83 shorter events, 0.6 us)
Async XLA Ops:
  7.2 0.9 copy-start
  7.2 49.8 %all-gather.3.cloned.1.call-start = ((), (), s32[]{:S(2)}) async-start(), calls=%async_computation.5 | async-start | bytes 1757184 | tf_op jit(solution)/shard_map/all_gather | solution.py:60
  8.8 161.3 %reduce-scatter.4.cloned.1.call-start = ((), (), s32[]{:S(2)}) async-start(), calls=%async_computation.6 | async-start | bytes 3514368
  86.2 5.2 copy-start.4
  86.2 90.0 %copy-start.2 = (bf16[1,208,6656]{2,1,0:T(8,128)(2,1)S(1)}, bf16[1,208,6656]{2,1,0:T(8,128)(2,1)}, u32[]{:S(2)}) copy-start(bf16[1,208,6656]{2,1,0:T(8,128)(2,1)} %param.13) | copy-start | bytes 8306692
  171.9 10.8 %all-to-all-start.1 = ((bf16[4,128,208]{1,2,0:T(8,128)(2,1)}), bf16[4,128,208]{1,2,0:T(8,128)(2,1)}, u32[]{:S(2)}, u32[]{:S(2)}) async-start(bf16[4,128,208]{1,2,0:T(8,128)(2,1)} %broadcast_in_dim.18), calls=%async_computation.1 | async-start | bytes 425984 | tf_op jit(solution)/shard_map/all_to_all | solution.py:13
  184.3 51.2 %all-gather.5.cloned.1.call-start = ((), (), s32[]{:S(2)}) async-start(), calls=%async_computation.7 | async-start | bytes 7028736 | tf_op jit(solution)/shard_map/while/body/eval_jaxpr/all_gather | solution.py:95
  235.6 6.8 %slice-start = ((s8[5537792]{0:T(1024)(128)(4,1)}), s8[4194304]{0:T(1024)(128)(4,1)S(1)}, s32[]{:S(2)}) async-start(s8[5537792]{0:T(1024)(128)(4,1)} %bitcast.45), calls=%async_computation.8 | async-start | bytes 8388608 | tf_op jit(solution)/shard_map/while
  235.6 6.8 %slice-start.2 = ((s8[6815744]{0:T(1024)(128)(4,1)}), s8[4194304]{0:T(1024)(128)(4,1)S(1)}, s32[]{:S(2)}) async-start(s8[6815744]{0:T(1024)(128)(4,1)} %bitcast.47), calls=%async_computation.10 | async-start | bytes 8388608 | tf_op jit(solution)/shard_map/while
  235.6 6.8 %slice-start.1 = ((s8[5537792]{0:T(1024)(128)(4,1)}), s8[1343488]{0:T(1024)(128)(4,1)S(1)}, s32[]{:S(2)}) async-start(s8[5537792]{0:T(1024)(128)(4,1)} %bitcast.45), calls=%async_computation.9 | async-start | bytes 2686976 | tf_op jit(solution)/shard_map/while
  235.6 6.8 %slice-start.3 = ((s8[6815744]{0:T(1024)(128)(4,1)}), s8[2621440]{0:T(1024)(128)(4,1)S(1)}, s32[]{:S(2)}) async-start(s8[6815744]{0:T(1024)(128)(4,1)} %bitcast.47), calls=%async_computation.11 | async-start | bytes 5242880 | tf_op jit(solution)/shard_map/while
  241.0 9.4 %collective-permute-start = (bf16[512,208]{0,1:T(8,128)(2,1)S(1)}, bf16[512,208]{0,1:T(8,128)(2,1)S(1)}, u32[]{:S(2)}, u32[]{:S(2)}) collective-permute-start(bf16[512,208]{0,1:T(8,128)(2,1)S(1)} %get-tuple-element.340), channel_id=1, source_target_pairs={{32,0},{64,32},{96,64},{33,1},{65,33},{97,65},{34,2},{66,34},{98,6... | collective-permute-start | bytes 638984 | tf_op jit(solution)/shard_map/while/body/eval_jaxpr/ppermute | solution.py:42
  245.9 4.5 copy-start.1
  250.4 0.7 copy-start.3
  251.1 52.3 %all-gather.5.cloned.1.call-start = ((), (), s32[]{:S(2)}) async-start(), calls=%async_computation.7 | async-start | bytes 7028736 | tf_op jit(solution)/shard_map/while/body/eval_jaxpr/all_gather | solution.py:95
  303.4 6.8 %slice-start = ((s8[5537792]{0:T(1024)(128)(4,1)}), s8[4194304]{0:T(1024)(128)(4,1)S(1)}, s32[]{:S(2)}) async-start(s8[5537792]{0:T(1024)(128)(4,1)} %bitcast.45), calls=%async_computation.8 | async-start | bytes 8388608 | tf_op jit(solution)/shard_map/while
  303.4 6.8 %slice-start.2 = ((s8[6815744]{0:T(1024)(128)(4,1)}), s8[4194304]{0:T(1024)(128)(4,1)S(1)}, s32[]{:S(2)}) async-start(s8[6815744]{0:T(1024)(128)(4,1)} %bitcast.47), calls=%async_computation.10 | async-start | bytes 8388608 | tf_op jit(solution)/shard_map/while
  303.4 6.8 %slice-start.1 = ((s8[5537792]{0:T(1024)(128)(4,1)}), s8[1343488]{0:T(1024)(128)(4,1)S(1)}, s32[]{:S(2)}) async-start(s8[5537792]{0:T(1024)(128)(4,1)} %bitcast.45), calls=%async_computation.9 | async-start | bytes 2686976 | tf_op jit(solution)/shard_map/while
  303.4 6.8 %slice-start.3 = ((s8[6815744]{0:T(1024)(128)(4,1)}), s8[2621440]{0:T(1024)(128)(4,1)S(1)}, s32[]{:S(2)}) async-start(s8[6815744]{0:T(1024)(128)(4,1)} %bitcast.47), calls=%async_computation.11 | async-start | bytes 5242880 | tf_op jit(solution)/shard_map/while
  308.8 9.4 %collective-permute-start = (bf16[512,208]{0,1:T(8,128)(2,1)S(1)}, bf16[512,208]{0,1:T(8,128)(2,1)S(1)}, u32[]{:S(2)}, u32[]{:S(2)}) collective-permute-start(bf16[512,208]{0,1:T(8,128)(2,1)S(1)} %get-tuple-element.340), channel_id=1, source_target_pairs={{32,0},{64,32},{96,64},{33,1},{65,33},{97,65},{34,2},{66,34},{98,6... | collective-permute-start | bytes 638984 | tf_op jit(solution)/shard_map/while/body/eval_jaxpr/ppermute | solution.py:42
  313.8 4.5 copy-start.1
  318.2 0.7 copy-start.3
  318.9 52.3 %all-gather.5.cloned.1.call-start = ((), (), s32[]{:S(2)}) async-start(), calls=%async_computation.7 | async-start | bytes 7028736 | tf_op jit(solution)/shard_map/while/body/eval_jaxpr/all_gather | solution.py:95
  371.3 6.8 %slice-start = ((s8[5537792]{0:T(1024)(128)(4,1)}), s8[4194304]{0:T(1024)(128)(4,1)S(1)}, s32[]{:S(2)}) async-start(s8[5537792]{0:T(1024)(128)(4,1)} %bitcast.45), calls=%async_computation.8 | async-start | bytes 8388608 | tf_op jit(solution)/shard_map/while
  371.3 6.8 %slice-start.2 = ((s8[6815744]{0:T(1024)(128)(4,1)}), s8[4194304]{0:T(1024)(128)(4,1)S(1)}, s32[]{:S(2)}) async-start(s8[6815744]{0:T(1024)(128)(4,1)} %bitcast.47), calls=%async_computation.10 | async-start | bytes 8388608 | tf_op jit(solution)/shard_map/while
  371.3 6.8 %slice-start.1 = ((s8[5537792]{0:T(1024)(128)(4,1)}), s8[1343488]{0:T(1024)(128)(4,1)S(1)}, s32[]{:S(2)}) async-start(s8[5537792]{0:T(1024)(128)(4,1)} %bitcast.45), calls=%async_computation.9 | async-start | bytes 2686976 | tf_op jit(solution)/shard_map/while
  371.3 6.8 %slice-start.3 = ((s8[6815744]{0:T(1024)(128)(4,1)}), s8[2621440]{0:T(1024)(128)(4,1)S(1)}, s32[]{:S(2)}) async-start(s8[6815744]{0:T(1024)(128)(4,1)} %bitcast.47), calls=%async_computation.11 | async-start | bytes 5242880 | tf_op jit(solution)/shard_map/while
  376.7 9.4 %collective-permute-start = (bf16[512,208]{0,1:T(8,128)(2,1)S(1)}, bf16[512,208]{0,1:T(8,128)(2,1)S(1)}, u32[]{:S(2)}, u32[]{:S(2)}) collective-permute-start(bf16[512,208]{0,1:T(8,128)(2,1)S(1)} %get-tuple-element.340), channel_id=1, source_target_pairs={{32,0},{64,32},{96,64},{33,1},{65,33},{97,65},{34,2},{66,34},{98,6... | collective-permute-start | bytes 638984 | tf_op jit(solution)/shard_map/while/body/eval_jaxpr/ppermute | solution.py:42
  381.6 4.5 copy-start.1
  386.1 0.7 copy-start.3
  386.8 52.3 %all-gather.5.cloned.1.call-start = ((), (), s32[]{:S(2)}) async-start(), calls=%async_computation.7 | async-start | bytes 7028736 | tf_op jit(solution)/shard_map/while/body/eval_jaxpr/all_gather | solution.py:95
  439.1 6.8 %slice-start = ((s8[5537792]{0:T(1024)(128)(4,1)}), s8[4194304]{0:T(1024)(128)(4,1)S(1)}, s32[]{:S(2)}) async-start(s8[5537792]{0:T(1024)(128)(4,1)} %bitcast.45), calls=%async_computation.8 | async-start | bytes 8388608 | tf_op jit(solution)/shard_map/while
  439.1 6.8 %slice-start.2 = ((s8[6815744]{0:T(1024)(128)(4,1)}), s8[4194304]{0:T(1024)(128)(4,1)S(1)}, s32[]{:S(2)}) async-start(s8[6815744]{0:T(1024)(128)(4,1)} %bitcast.47), calls=%async_computation.10 | async-start | bytes 8388608 | tf_op jit(solution)/shard_map/while
  439.1 6.8 %slice-start.1 = ((s8[5537792]{0:T(1024)(128)(4,1)}), s8[1343488]{0:T(1024)(128)(4,1)S(1)}, s32[]{:S(2)}) async-start(s8[5537792]{0:T(1024)(128)(4,1)} %bitcast.45), calls=%async_computation.9 | async-start | bytes 2686976 | tf_op jit(solution)/shard_map/while
  439.1 6.8 %slice-start.3 = ((s8[6815744]{0:T(1024)(128)(4,1)}), s8[2621440]{0:T(1024)(128)(4,1)S(1)}, s32[]{:S(2)}) async-start(s8[6815744]{0:T(1024)(128)(4,1)} %bitcast.47), calls=%async_computation.11 | async-start | bytes 5242880 | tf_op jit(solution)/shard_map/while
  444.5 9.4 %collective-permute-start = (bf16[512,208]{0,1:T(8,128)(2,1)S(1)}, bf16[512,208]{0,1:T(8,128)(2,1)S(1)}, u32[]{:S(2)}, u32[]{:S(2)}) collective-permute-start(bf16[512,208]{0,1:T(8,128)(2,1)S(1)} %get-tuple-element.340), channel_id=1, source_target_pairs={{32,0},{64,32},{96,64},{33,1},{65,33},{97,65},{34,2},{66,34},{98,6... | collective-permute-start | bytes 638984 | tf_op jit(solution)/shard_map/while/body/eval_jaxpr/ppermute | solution.py:42
  449.4 4.5 copy-start.1
  453.9 0.7 copy-start.3
  454.6 4.5 copy-start.6
  454.6 13.3 %copy-start.5 = (f32[1,6656]{1,0:T(1,128)S(1)}, f32[1,6656]{1,0:T(1,128)}, u32[]{:S(2)}) copy-start(f32[1,6656]{1,0:T(1,128)} %param.15) | copy-start | bytes 79876
  463.0 19.7 %all-to-all-start.2 = ((f32[32,1,6658]{2,1,0:T(1,128)}), f32[32,1,6658]{2,1,0:T(1,128)}, u32[]{:S(2)}, u32[]{:S(2)}) async-start(f32[32,1,6658]{2,1,0:T(1,128)} %broadcast_in_dim.20), calls=%async_computation.2 | async-start | bytes 1736704 | tf_op jit(solution)/shard_map/all_to_all | solution.py:13
  492.2 11.5 %all-to-all-start.3 = ((f32[32,1,1]{2,1,0:T(1,128)}), f32[32,1,1]{2,1,0:T(1,128)S(1)}, u32[]{:S(2)}, u32[]{:S(2)}) async-start(f32[32,1,1]{2,1,0:T(1,128)} %broadcast_in_dim.21), calls=%async_computation.3 | async-start | bytes 32768 | tf_op jit(solution)/shard_map/all_to_all | solution.py:13
Sparse Core Ops, SparseCore 0:
  10.9 46.0 all-gather.2
  91.4 78.5 reduce-scatter.3
  188.0 47.5 all-gather.4
  254.4 48.9 all-gather.4
  322.3 48.9 all-gather.4
  390.1 48.9 all-gather.4
where the time goes:
time: 520 us; the launch traced here: 518 us
  waiting for transfers between devices  361 us (69%)
  matrix products  51.5 us (10%)
  other arithmetic  27.9 us (5%)
  blocking collectives  22.3 us (4%)
  local copies, waits for them, and re-layouts  19 us (4%)
  starting transfers between devices  19 us (4%)
  between operations  17.3 us (3%)
    all_gather x4, waiting for transfers between devices, layer_block(): gathered = lax.all_gather(dy_rows, 'tensor', axis=1, tiled=True)  202 us
    unnamed x3, waiting for transfers between devices  78.6 us
    all_gather x1, waiting for transfers between devices, body(): lax.all_gather(hidden_rows, 'tensor', axis=1, tiled=True)  47.4 us
    dot_general x4, matrix products, layer_block(): lax.dot_general(gathered, local_weight, (((1,), (1,)), ((), ())), preferr...  21.5 us
    ppermute x4, waiting for transfers between devices, shifted(): return lax.ppermute(block, axis, route)  17.8 us
    all_to_all x3, waiting for transfers between devices, copy_for_each(): lax.all_to_all(jnp.broadcast_to(x[None], (peers, *x.shape)), axis, 0, 0,...  15.3 us
    dot_general x4, matrix products, layer_block(): lax.dot_general(saved_rows, gathered, (((0,), (0,)), ((), ())), preferred...  13.9 us
    all_to_all x3, starting transfers between devices, copy_for_each(): lax.all_to_all(jnp.broadcast_to(x[None], (peers, *x.shape)), axis, 0, 0,...  13.3 us
  transfers between devices with their start and end apart: 13, of which 13 were waited for; matrix products, arithmetic and copies ran while one was open for 3% of the time, Pallas kernels for 0%

commit v1 on v0

v1 whole, which is shorter than its diff:
```python
import jax
import jax.numpy as jnp
from jax import lax
from jax.sharding import Mesh, PartitionSpec as P

decay_rate = 0.9
learn_rate = 0.3
tiny_term = 1e-30
bf16_largest = 3.3895e38


def from_ring(block, axis):
    size = lax.axis_size(axis)
    return [block] + [
        lax.ppermute(block, axis, [(i, (i - step) % size) for i in range(size)])
        for step in range(1, size)
    ]


def rotated(pieces, index, axis=0):
    count = len(pieces)
    placed = []
    for k in range(count):
        chosen = pieces[k]
        for shift in range(1, count):
            chosen = jnp.where(index == shift, pieces[(k - shift) % count], chosen)
        placed.append(chosen)
    return jnp.stack(placed, axis=axis)


def gathered(block, axis, at=0):
    return rotated(from_ring(block, axis), lax.axis_index(axis), at)


def gathered_tensor(block):
    return gathered(gathered(gathered(block, "z"), "y"), "c", 2).reshape(-1, block.shape[-1])


def summed(x, axis):
    pieces = from_ring(x, axis)
    if len(pieces) == 2:
        return pieces[0] + pieces[1]
    return (pieces[0] + pieces[2]) + (pieces[1] + pieces[3])


def summed_tensor(x):
    return summed(summed(summed(x, "c"), "z"), "y")


def scattered(blocks, axis):
    size = lax.axis_size(axis)
    index = lax.axis_index(axis)
    total = None
    for step in range(size):
        piece = blocks[step]
        for shift in range(1, size):
            piece = jnp.where(index == shift, blocks[(step + shift) % size], piece)
        if step:
            piece = lax.ppermute(
                piece.astype(jnp.bfloat16), axis, [(i, (i + step) % size) for i in range(size)]
            )
        piece = piece.astype(jnp.float32)
        total = piece if total is None else total + piece
    return total


def body(hidden_last, labels, head_weight, layer_inputs, weights, row_state, col_state):
    section_count = lax.axis_size("x")
    section_index = lax.axis_index("x")
    core = lax.axis_index("c")
    all_rows = labels.shape[0]
    model_width, vocab_local = head_weight.shape
    local_weight = weights[0]
    rows_local = local_weight.shape[0]
    saved_all = layer_inputs[0]
    tensor_index = lax.axis_index(("y", "z", "c"))
    columns = tensor_index * vocab_local + lax.iota(jnp.int32, vocab_local)
    share = all_rows // section_count
    row_start = section_index * share
    entries = float(model_width * model_width)

    hidden_rows = lax.dynamic_slice_in_dim(hidden_last, row_start, share, 0).T
    hidden_all = gathered_tensor(hidden_rows)
    logits = lax.dot_general(
        head_weight, hidden_all, (((0,), (0,)), ((), ())), preferred_element_type=jnp.float32
    )
    exponent = jnp.exp(logits)
    label_hit = lax.dynamic_slice_in_dim(labels, row_start, share, 0)[None, :] == columns[:, None]
    weight_float = local_weight.astype(jnp.float32)
    weight_part = jnp.broadcast_to(jnp.sum(weight_float * weight_float), (share,))
    sums = summed_tensor(
        jnp.stack(
            [
                jnp.sum(exponent, axis=0),
                jnp.sum(jnp.where(label_hit, logits, jnp.zeros_like(logits)), axis=0),
                weight_part,
            ]
        )
    )
    denominator, picked, weight_total = sums[0], sums[1], sums[2, 0]
    both = jnp.concatenate(
        [jnp.minimum(exponent, bf16_largest).astype(jnp.bfloat16), label_hit.astype(jnp.bfloat16)], axis=1
    )
    product = jnp.dot(head_weight, both, preferred_element_type=jnp.float32)
    part = (product[:, :share] / denominator[None, :] - product[:, share:]) / all_rows
    part = part.reshape(4, 4, 2, rows_local, share)
    part = scattered([part[:, :, 0], part[:, :, 1]], "c")
    part = scattered(part, "y")
    part = scattered(part, "z")
    head_grad = gathered(part.astype(jnp.bfloat16), "x", 1).reshape(rows_local, all_rows)
    loss = summed(jnp.sum(jnp.log(denominator) - picked)[None], "x")[0] / all_rows

    dy = head_grad
    outputs = jnp.zeros((rows_local, all_rows), jnp.bfloat16)
    gradient = jnp.zeros((rows_local, model_width), jnp.float32)
    for step in range(4):
        active = step == section_count - 1 - section_index
        full = lax.all_gather(dy, ("y", "z", "c"), axis=0, tiled=True)
        backward = jnp.dot(local_weight, full, preferred_element_type=jnp.float32)
        input_grad = (dy.astype(jnp.float32) + backward).astype(jnp.bfloat16)
        outputs = jnp.where(active, input_grad, outputs)
        if step < 3:
            dy = lax.ppermute(input_grad, "x", [(i, i - 1) for i in range(1, 4)])
        gradient = lax.cond(
            active,
            lambda g, f: lax.dot_general(
                saved_all, f, (((0,), (1,)), ((), ())), preferred_element_type=jnp.float32
            ),
            lambda g, f: g,
            gradient,
            full,
        )

    squares = gradient * gradient
    row_new = decay_rate * row_state[0] + (1.0 - decay_rate) * jnp.mean(squares + tiny_term, axis=1)
    col_part = jnp.sum(squares + tiny_term, axis=0)
    scaled_part = jnp.sum(squares * (1.0 / row_new)[:, None], axis=0)
    row_part = jnp.broadcast_to(jnp.sum(row_new), (128,))
    payload = jnp.concatenate([col_part, scaled_part, row_part]).reshape(-1, 128)
    payload = summed_tensor(payload).reshape(-1)
    col_sum = payload[:model_width]
    scaled_sum = payload[model_width : 2 * model_width]
    row_total = payload[2 * model_width]
    col_new = decay_rate * col_state[0] + (1.0 - decay_rate) * (col_sum / model_width)
    update_total = row_total * jnp.sum(scaled_sum / col_new)
    factor = (
        learn_rate
        * jnp.sqrt(weight_total / entries)
        / jnp.maximum(1.0, jnp.sqrt(update_total / entries))
    )
    row_scale = factor * jnp.sqrt(row_total / row_new)
    col_scale = 1.0 / jnp.sqrt(col_new)
    new_weight = (weight_float - gradient * row_scale[:, None] * col_scale[None, :]).astype(jnp.bfloat16)
    return (loss, outputs.T[None], new_weight[None], row_new[None], col_new[None])


def solution(mesh):
    fine = Mesh(mesh.devices.reshape(4, 4, 4, 2), ("x", "y", "z", "c"))
    tensor = ("y", "z", "c")
    return jax.shard_map(
        body,
        mesh=fine,
        in_specs=(
            P(None, tensor),
            P(),
            P(None, tensor),
            P("x", None, tensor),
            P("x", tensor, None),
            P("x", tensor),
            P("x", None),
        ),
        out_specs=(
            P(),
            P("x", None, tensor),
            P("x", tensor, None),
            P("x", tensor),
            P("x", None),
        ),
        check_vma=False,
    )
```

time: 520 us -> 412 us (0.79)
  waiting for transfers between devices: 361 us -> 256 us
  starting transfers between devices: 19 us -> 51.4 us
  blocking collectives: 22.3 us -> 0 us
  matrix products: 51.5 us -> 42.8 us
    unnamed x3 -> x4, waiting for transfers between devices: 78.6 us -> 0.07 us
    all_gather x5 -> x4, waiting for transfers between devices: 249 us -> 194 us  [body(): full = lax.all_gather(dy, ('y', 'z', 'c'), axis=0, tiled=True)]
    ppermute x4 -> x37, starting transfers between devices: 5.65 us -> 51.3 us  [the longest x27 37.6 us: from_ring(): lax.ppermute(block, axis, [(i, (i - step) % size) for i in range(size)])]
    ppermute x4 -> x37, waiting for transfers between devices: 17.8 us -> 61.5 us  [the longest x3 24 us: body(): dy = lax.ppermute(input_grad, 'x', [(i, i - 1) for i in range(1, 4)])]
    all_to_all x3 -> x0, waiting for transfers between devices: 15.3 us -> none  [copy_for_each(): lax.all_to_all(jnp.broadcast_to(x[None], (peers, *x.shape)), axis, 0, 0,...]
    all_to_all x3 -> x0, starting transfers between devices: 13.3 us -> none  [copy_for_each(): lax.all_to_all(jnp.broadcast_to(x[None], (peers, *x.shape)), axis, 0, 0,...]
    all_to_all x1 -> x0, blocking collectives: 12.4 us -> none  [copy_for_each(): lax.all_to_all(jnp.broadcast_to(x[None], (peers, *x.shape)), axis, 0, 0,...]
    psum x1 -> x0, blocking collectives: 9.88 us -> none  [body(): loss = lax.psum(part_loss, 'section') / all_rows]
  transfers between devices with their start and end apart: 13 -> 41, of which waited for: 13 -> 25; matrix products, arithmetic and copies ran while one was open for 3% -> 5% of each run, Pallas kernels for 0% -> 0%
where the time goes in v1:
time: 412 us; the launch traced here: 410 us
  waiting for transfers between devices  256 us (62%)
  starting transfers between devices  51.4 us (12%)
  matrix products  42.8 us (10%)
  other arithmetic  25.7 us (6%)
  between operations  20 us (5%)
  local copies, waits for them, and re-layouts  14.9 us (4%)
    all_gather x4, waiting for transfers between devices, body(): full = lax.all_gather(dy, ('y', 'z', 'c'), axis=0, tiled=True)  194 us
    ppermute x27, starting transfers between devices, from_ring(): lax.ppermute(block, axis, [(i, (i - step) % size) for i in range(size)])  37.6 us
    ppermute x3, waiting for transfers between devices, body(): dy = lax.ppermute(input_grad, 'x', [(i, i - 1) for i in range(1, 4)])  24 us
    ppermute x27, waiting for transfers between devices, from_ring(): lax.ppermute(block, axis, [(i, (i - step) % size) for i in range(size)])  22.7 us
    dot_general x4, matrix products, body(): backward = jnp.dot(local_weight, full, preferred_element_type=jnp.float32)  19.7 us
    ppermute x7, waiting for transfers between devices, scattered(): lax.ppermute(piece.astype(jnp.bfloat16), axis, [(i, (i + step) % size) fo...  14.8 us
    ppermute x7, starting transfers between devices, scattered(): lax.ppermute(piece.astype(jnp.bfloat16), axis, [(i, (i + step) % size) fo...  9.78 us
    dot_general x1, matrix products, body(): lax.dot_general(head_weight, hidden_all, (((0,), (0,)), ((), ())), prefer...  8.39 us
  transfers between devices with their start and end apart: 41, of which 25 were waited for; matrix products, arithmetic and copies ran while one was open for 5% of the time, Pallas kernels for 0%

profile of v1, /device:TPU:0, one launch (start us, length us, event | category | flops | bytes accessed | tf_op | source)
XLA Modules:
  0.0 410.4 jit_solution(6000275937418690555)
XLA Ops:
  7.2 1.0 dynamic-slice_bitcast_fusion
  8.2 2.0 collective-permute-start.2
  10.2 3.6 collective-permute-start.1
  13.8 1.0 collective-permute-start
  14.8 1.7 collective-permute-done.1
  16.5 1.4 collective-permute-done
  17.9 0.9 select_bitcast_fusion.13
  20.2 1.6 collective-permute-start.5
  21.7 2.9 collective-permute-start.4
  24.6 1.3 collective-permute-start.3
  26.0 3.1 collective-permute-done.5
  29.1 3.9 collective-permute-done.4
  34.3 0.9 select_bitcast_fusion.4
  35.2 1.3 select_bitcast_fusion.5
  36.6 1.0 pad_maximum_fusion.1
  38.4 2.0 fusion
  41.1 1.3 select_bitcast_fusion.1
  42.6 8.4 %exponential_reduce_fusion = (f32[128]{0:T(128)S(1)}, f32[128]{0:T(128)S(1)}, bf16[1000,128]{1,0:T(8,128)(2,1)S(1)}) fusion(s32[1000]{0:T(1024)S(1)} %iota_add_fusion, s32[128]{0:T(128)S(1)} %dynamic_slice.7, bf16[6656,128]{1,0:T(8,128)(2,1)S(1)} %bitcast.251, bf16[6656,1000]{0,1:T(8,128)(2,1)} %param.17), kind=kOutput, calls=%fused_computation.43 | convolution fusion | flops 1704703744 | bytes 15277472 | tf_op jit(solution)/shard_map/dot_general | solution.py:84
  52.5 2.0 collective-permute-start.9
  54.5 1.5 collective-permute-start.8
  56.3 3.0 collective-permute-done.10
  60.2 2.8 collective-permute-start.12
  63.6 7.0 %convolution_bitcast_fusion = f32[6656,256]{0,1:T(8,128)S(1)} fusion(bf16[6656,1000]{0,1:T(8,128)(2,1)} %param.17, bf16[1000,128]{1,0:T(8,128)(2,1)S(1)} %compare_convert_fusion, bf16[1000,128]{1,0:T(8,128)(2,1)S(1)} %get-tuple-element.58), kind=kOutput, calls=%fused_computation | convolution fusion | flops 3408896000 | bytes 20639744 | tf_op jit(solution)/shard_map/dot_general | solution.py:104
  70.7 2.2 fusion.2
  73.0 3.6 copy.17
  76.8 2.4 collective-permute-done.17
  79.9 2.9 collective-permute-start.20
  82.8 1.6 collective-permute-start.19
  84.5 8.2 %collective-permute-done.18 = bf16[4,208,128]{2,1,0:T(8,128)(2,1)S(1)} collective-permute-done((bf16[4,208,128]{2,1,0:T(8,128)(2,1)S(1)}, bf16[4,208,128]{2,1,0:T(8,128)(2,1)S(1)}, u32[]{:S(2)}, u32[]{:S(2)}) %collective-permute-start.18) | collective-permute-done | bytes 213024 | tf_op jit(solution)/shard_map/ppermute | solution.py:59
  93.5 2.8 collective-permute-start.23
  96.2 1.4 collective-permute-start.22
  98.5 3.4 collective-permute-done.22
  101.9 1.6 collective-permute-start.26
  103.5 2.7 collective-permute-start.25
  106.2 1.4 collective-permute-start.24
  107.7 1.5 collective-permute-done.25
  109.1 1.2 collective-permute-done.24
  111.2 49.9 %all-gather.5.cloned.1.call-done = bf16[6656,512]{1,0:T(8,128)(2,1)} async-done(((bf16[208,512]{1,0:T(8,128)(2,1)}), bf16[6656,512]{1,0:T(8,128)(2,1)}) %all-gather.5.cloned.1.call-update) | async-done | bytes 6815760 | tf_op jit(solution)/shard_map/all_gather | solution.py:118
  161.2 5.4 %fusion.27 = bf16[208,512]{1,0:T(8,128)(2,1)S(1)} fusion(bf16[6656,512]{1,0:T(8,128)(2,1)} %all-gather.5.cloned.1.call-done, bf16[1,208,6656]{2,1,0:T(8,128)(2,1)} %param.19, bf16[208,1,128]{2,0,1:T(8,128)(2,1)S(1)} %get-tuple-element.63, bf16[208,1,128]{2,0,1:T(8,128)(2,1)S(1)} %get-tuple-element.64, bf16[208,1,128]{2,0,1:T(8,128)(2,1)S(1)} %get-tuple-element.65, ...), kind=kOutput, calls=%fused_computation.31 | convolution fusion | flops 1418313728 | bytes 10010624 | tf_op jit(solution)/shard_map/dot_general | solution.py:119
  166.6 1.3 collective-permute-start.27
  167.9 8.0 %collective-permute-done.27 = bf16[208,512]{1,0:T(8,128)(2,1)S(1)} collective-permute-done((bf16[208,512]{1,0:T(8,128)(2,1)S(1)}, bf16[208,512]{1,0:T(8,128)(2,1)S(1)}, u32[]{:S(2)}, u32[]{:S(2)}) %collective-permute-start.27) | collective-permute-done | bytes 213024 | tf_op jit(solution)/shard_map/ppermute | solution.py:123
  176.6 49.1 %all-gather.7.cloned.1.call-done = bf16[6656,512]{1,0:T(8,128)(2,1)} async-done(((bf16[208,512]{1,0:T(8,128)(2,1)}), bf16[6656,512]{1,0:T(8,128)(2,1)}) %all-gather.7.cloned.1.call-update) | async-done | bytes 6815760 | tf_op jit(solution)/shard_map/all_gather | solution.py:118
  225.7 4.5 %add_convert_fusion.2 = bf16[208,512]{1,0:T(8,128)(2,1)S(1)} fusion(bf16[208,512]{1,0:T(8,128)(2,1)} %copy-done.12, bf16[6656,512]{1,0:T(8,128)(2,1)} %all-gather.7.cloned.1.call-done, bf16[1,208,6656]{2,1,0:T(8,128)(2,1)S(1)} %copy-done.2), kind=kOutput, calls=%fused_computation.50 | convolution fusion | flops 1417994240 | bytes 10010624 | tf_op jit(solution)/shard_map/dot_general | solution.py:119
  230.2 1.3 collective-permute-start.28
  231.5 8.0 %collective-permute-done.28 = bf16[208,512]{1,0:T(8,128)(2,1)S(1)} collective-permute-done((bf16[208,512]{1,0:T(8,128)(2,1)S(1)}, bf16[208,512]{1,0:T(8,128)(2,1)S(1)}, u32[]{:S(2)}, u32[]{:S(2)}) %collective-permute-start.28) | collective-permute-done | bytes 213024 | tf_op jit(solution)/shard_map/ppermute | solution.py:123
  240.3 49.1 %all-gather.9.cloned.1.call-done = bf16[6656,512]{1,0:T(8,128)(2,1)} async-done(((bf16[208,512]{1,0:T(8,128)(2,1)}), bf16[6656,512]{1,0:T(8,128)(2,1)}) %all-gather.9.cloned.1.call-update) | async-done | bytes 6815760 | tf_op jit(solution)/shard_map/all_gather | solution.py:118
  289.4 4.5 %add_convert_fusion.1 = bf16[208,512]{1,0:T(8,128)(2,1)S(1)} fusion(bf16[208,512]{1,0:T(8,128)(2,1)} %copy-done.13, bf16[6656,512]{1,0:T(8,128)(2,1)} %all-gather.9.cloned.1.call-done, bf16[1,208,6656]{2,1,0:T(8,128)(2,1)S(1)} %copy-done.2), kind=kOutput, calls=%fused_computation.49 | convolution fusion | flops 1417994240 | bytes 10010624 | tf_op jit(solution)/shard_map/dot_general | solution.py:119
  293.9 1.3 collective-permute-start.29
  295.2 8.0 %collective-permute-done.29 = bf16[208,512]{1,0:T(8,128)(2,1)S(1)} collective-permute-done((bf16[208,512]{1,0:T(8,128)(2,1)S(1)}, bf16[208,512]{1,0:T(8,128)(2,1)S(1)}, u32[]{:S(2)}, u32[]{:S(2)}) %collective-permute-start.29) | collective-permute-done | bytes 213024 | tf_op jit(solution)/shard_map/ppermute | solution.py:123
  304.1 3.0 conditional.4
  304.1 3.0 broadcast_in_dim.0
  307.1 45.9 %all-gather.11.cloned.1.call-done = bf16[6656,512]{1,0:T(8,128)(2,1)} async-done(((bf16[208,512]{1,0:T(8,128)(2,1)}), bf16[6656,512]{1,0:T(8,128)(2,1)}) %all-gather.11.cloned.1.call-update) | async-done | bytes 6815760 | tf_op jit(solution)/shard_map/all_gather | solution.py:118
  353.0 7.7 %conditional.7 = (f32[208,6656]{1,0:T(8,128)}) conditional(s32[]{:T(128)} %convert_element_type.123, f32[208,6656]{1,0:T(8,128)} %get-tuple-element.78, (bf16[512,208]{1,0:T(8,128)(2,1)S(1)}, bf16[6656,512]{1,0:T(8,128)(2,1)}) %tuple.77), branch_computations={%region_10.11_spmd, %region_11.12_spmd} | conditional | flops 1417674752 | bytes 12566536 | solution.py:124
  353.0 7.7 %fusion.51 = f32[208,6656]{1,0:T(8,128)} fusion(bf16[512,208]{1,0:T(8,128)(2,1)S(1)} %get-tuple-element.37, bf16[6656,512]{1,0:T(8,128)(2,1)} %get-tuple-element.38), kind=kOutput, calls=%fused_computation.112 | convolution fusion | flops 1417674752 | bytes 12566528 | tf_op jit(solution)/shard_map/cond/branch_1_fun/dot_general | solution.py:126
  360.8 3.4 add_reduce_fusion
  365.3 1.0 add_reduce_fusion.1
  367.4 0.9 collective-permute-done.30
  368.3 1.9 collective-permute-start.32
  370.4 2.1 collective-permute-start.31
  374.3 4.6 %collective-permute-done.14 = f32[1]{0:T(128)} collective-permute-done((f32[1]{0:T(128)}, f32[1]{0:T(128)}, u32[]{:S(2)}, u32[]{:S(2)}) %collective-permute-start.14) | collective-permute-done | bytes 36 | tf_op jit(solution)/shard_map/ppermute | solution.py:15
  378.9 3.2 collective-permute-start.15
  385.1 3.1 collective-permute-start.35
  388.6 5.2 %fusion.36 = bf16[1,512,208]{1,2,0:T(8,128)(2,1)} fusion(bf16[208,512]{1,0:T(8,128)(2,1)S(1)} %copy-done.11, bf16[208,512]{1,0:T(8,128)(2,1)S(1)} %copy-done.21, bf16[208,512]{1,0:T(8,128)(2,1)S(1)} %copy-done.19, bf16[208,512]{1,0:T(8,128)(2,1)S(1)} %copy-done.17, pred[]{:T(512)S(6)} %eq.50, pred[]{:T(512)S(6)} %eq.49, pred[]{:T(512)S(6)} %eq.48, ...), kind=kOutput, calls=%fused_computation.56 | convolution fusion | flops 1418420224 | bytes 10649604 | tf_op jit(solution)/shard_map/dot_general | solution.py:119
  397.7 5.0 %fusion.3 = bf16[1,208,6656]{2,1,0:T(8,128)(2,1)} fusion(f32[208,6656]{1,0:T(8,128)} %get-tuple-element.79, bf16[1,208,6656]{2,1,0:T(8,128)(2,1)S(1)} %copy-done.2, f32[6656]{0:T(1024)S(1)} %get-tuple-element.48, f32[208]{0:T(256)S(1)} %sqrt_multiply_fusion), kind=kLoop, calls=%fused_computation.11 | loop fusion | flops 6922240 | bytes 11103040 | tf_op jit(solution)/shard_map/broadcast_in_dim | solution.py:154
  (125 shorter events, 20.5 us)
Async XLA Ops:
  7.2 31.2 %copy-start.1 = (bf16[1,208,6656]{2,1,0:T(8,128)(2,1)S(1)}, bf16[1,208,6656]{2,1,0:T(8,128)(2,1)}, u32[]{:S(2)}) copy-start(bf16[1,208,6656]{2,1,0:T(8,128)(2,1)} %param.19) | copy-start | bytes 8306692
  7.2 154.0 %all-gather.5.cloned.1.call-start = ((), (), s32[]{:S(2)}) async-start(), calls=%async_computation | async-start | bytes 7028736 | tf_op jit(solution)/shard_map/all_gather | solution.py:118
  8.2 6.6 %collective-permute-start.2 = (bf16[208,128]{1,0:T(8,128)(2,1)S(1)}, bf16[208,128]{1,0:T(8,128)(2,1)S(1)}, u32[]{:S(2)}, u32[]{:S(2)}) collective-permute-start(bf16[208,128]{1,0:T(8,128)(2,1)S(1)} %dynamic-slice_bitcast_fusion), channel_id=1, source_target_pairs={{0,2},{2,4},{4,6},{6,0},{1,3},{3,5},{5,7},{7,1},{8,10},{10,12},{12... | collective-permute-start | bytes 159752 | tf_op jit(solution)/shard_map/ppermute | solution.py:15
  10.2 6.3 %collective-permute-start.1 = (bf16[208,128]{1,0:T(8,128)(2,1)S(1)}, bf16[208,128]{1,0:T(8,128)(2,1)S(1)}, u32[]{:S(2)}, u32[]{:S(2)}) collective-permute-start(bf16[208,128]{1,0:T(8,128)(2,1)S(1)} %dynamic-slice_bitcast_fusion), channel_id=1, source_target_pairs={{0,4},{2,6},{4,0},{6,2},{1,5},{3,7},{5,1},{7,3},{8,12},{10,14},{12... | collective-permute-start | bytes 159752 | tf_op jit(solution)/shard_map/ppermute | solution.py:15
  13.8 4.1 %collective-permute-start = (bf16[208,128]{1,0:T(8,128)(2,1)S(1)}, bf16[208,128]{1,0:T(8,128)(2,1)S(1)}, u32[]{:S(2)}, u32[]{:S(2)}) collective-permute-start(bf16[208,128]{1,0:T(8,128)(2,1)S(1)} %dynamic-slice_bitcast_fusion), channel_id=1, source_target_pairs={{0,6},{2,0},{4,2},{6,4},{1,7},{3,1},{5,3},{7,5},{8,14},{10,8},{12,... | collective-permute-start | bytes 159752 | tf_op jit(solution)/shard_map/ppermute | solution.py:15
  18.8 0.6 copy-start.7
  18.8 0.6 copy-start.8
  20.2 8.9 %collective-permute-start.5 = (bf16[4,208,128]{2,1,0:T(8,128)(2,1)}, bf16[4,208,128]{2,1,0:T(8,128)(2,1)S(1)}, u32[]{:S(2)}, u32[]{:S(2)}) collective-permute-start(bf16[4,208,128]{2,1,0:T(8,128)(2,1)} %pad_maximum_fusion.2), channel_id=1, source_target_pairs={{0,8},{8,16},{16,24},{24,0},{1,9},{9,17},{17,25},{25,1},{2,10},{10... | collective-permute-start | bytes 638984 | tf_op jit(solution)/shard_map/ppermute | solution.py:15
  21.7 11.2 %collective-permute-start.4 = (bf16[4,208,128]{2,1,0:T(8,128)(2,1)}, bf16[4,208,128]{2,1,0:T(8,128)(2,1)S(1)}, u32[]{:S(2)}, u32[]{:S(2)}) collective-permute-start(bf16[4,208,128]{2,1,0:T(8,128)(2,1)} %pad_maximum_fusion.2), channel_id=1, source_target_pairs={{0,16},{8,24},{16,0},{24,8},{1,17},{9,25},{17,1},{25,9},{2,18},{10... | collective-permute-start | bytes 638984 | tf_op jit(solution)/shard_map/ppermute | solution.py:15
  24.6 8.3 %collective-permute-start.3 = (bf16[4,208,128]{2,1,0:T(8,128)(2,1)}, bf16[4,208,128]{2,1,0:T(8,128)(2,1)S(1)}, u32[]{:S(2)}, u32[]{:S(2)}) collective-permute-start(bf16[4,208,128]{2,1,0:T(8,128)(2,1)} %pad_maximum_fusion.2), channel_id=1, source_target_pairs={{0,24},{8,0},{16,8},{24,16},{1,25},{9,1},{17,9},{25,17},{2,26},{10... | collective-permute-start | bytes 638984 | tf_op jit(solution)/shard_map/ppermute | solution.py:15
  29.1 3.9 copy-start.4
  33.0 0.7 copy-start.5
  33.7 0.7 copy-start.6
  35.2 1.3 copy-start.3
  37.6 3.5 collective-permute-start.6
  51.1 1.4 collective-permute-start.7
  52.5 3.8 collective-permute-start.9
  54.5 4.8 %collective-permute-start.10 = (f32[3,128]{1,0:T(4,128)S(1)}, f32[3,128]{1,0:T(4,128)S(1)}, u32[]{:S(2)}, u32[]{:S(2)}) collective-permute-start(f32[3,128]{1,0:T(4,128)S(1)} %fusion.44), channel_id=1, source_target_pairs={{0,2},{2,4},{4,6},{6,0},{1,3},{3,5},{5,7},{7,1},{8,10},{10,12},{12... | collective-permute-start | bytes 4616 | tf_op jit(solution)/shard_map/ppermute | solution.py:15
  54.5 5.1 %collective-permute-start.8 = (f32[3,128]{1,0:T(4,128)S(1)}, f32[3,128]{1,0:T(4,128)S(1)}, u32[]{:S(2)}, u32[]{:S(2)}) collective-permute-start(f32[3,128]{1,0:T(4,128)S(1)} %fusion.44), channel_id=1, source_target_pairs={{0,4},{2,6},{4,0},{6,2},{1,5},{3,7},{5,1},{7,3},{8,12},{10,14},{12... | collective-permute-start | bytes 4616 | tf_op jit(solution)/shard_map/ppermute | solution.py:15
  59.7 11.0 %collective-permute-start.13 = (f32[3,128]{1,0:T(4,128)S(1)}, f32[3,128]{1,0:T(4,128)S(1)}, u32[]{:S(2)}, u32[]{:S(2)}) collective-permute-start(f32[3,128]{1,0:T(4,128)S(1)} %add_add_fusion.3), channel_id=1, source_target_pairs={{0,8},{8,16},{16,24},{24,0},{1,9},{9,17},{17,25},{25,1},{2,10},{10... | collective-permute-start | bytes 4616 | tf_op jit(solution)/shard_map/ppermute | solution.py:15
  60.2 10.5 %collective-permute-start.12 = (f32[3,128]{1,0:T(4,128)S(1)}, f32[3,128]{1,0:T(4,128)S(1)}, u32[]{:S(2)}, u32[]{:S(2)}) collective-permute-start(f32[3,128]{1,0:T(4,128)S(1)} %add_add_fusion.3), channel_id=1, source_target_pairs={{0,24},{8,0},{16,8},{24,16},{1,25},{9,1},{17,9},{25,17},{2,26},{10... | collective-permute-start | bytes 4616 | tf_op jit(solution)/shard_map/ppermute | solution.py:15
  62.9 7.8 %collective-permute-start.11 = (f32[3,128]{1,0:T(4,128)S(1)}, f32[3,128]{1,0:T(4,128)S(1)}, u32[]{:S(2)}, u32[]{:S(2)}) collective-permute-start(f32[3,128]{1,0:T(4,128)S(1)} %add_add_fusion.3), channel_id=1, source_target_pairs={{0,16},{8,24},{16,0},{24,8},{1,17},{9,25},{17,1},{25,9},{2,18},{10... | collective-permute-start | bytes 4616 | tf_op jit(solution)/shard_map/ppermute | solution.py:15
  76.7 2.5 collective-permute-start.17
  79.5 13.1 %collective-permute-start.18 = (bf16[4,208,128]{2,1,0:T(8,128)(2,1)S(1)}, bf16[4,208,128]{2,1,0:T(8,128)(2,1)S(1)}, u32[]{:S(2)}, u32[]{:S(2)}) collective-permute-start(bf16[4,208,128]{2,1,0:T(8,128)(2,1)S(1)} %get-tuple-element.50), channel_id=1, source_target_pairs={{0,8},{8,16},{16,24},{24,0},{1,9},{9,17},{17,25},{25,1},{2,10},{10... | collective-permute-start | bytes 638984 | tf_op jit(solution)/shard_map/ppermute | solution.py:59
  79.9 12.7 %collective-permute-start.20 = (bf16[4,208,128]{2,1,0:T(8,128)(2,1)S(1)}, bf16[4,208,128]{2,1,0:T(8,128)(2,1)S(1)}, u32[]{:S(2)}, u32[]{:S(2)}) collective-permute-start(bf16[4,208,128]{2,1,0:T(8,128)(2,1)S(1)} %get-tuple-element.51), channel_id=1, source_target_pairs={{0,24},{8,0},{16,8},{24,16},{1,25},{9,1},{17,9},{25,17},{2,26},{10... | collective-permute-start | bytes 638984 | tf_op jit(solution)/shard_map/ppermute | solution.py:59
  82.8 9.8 %collective-permute-start.19 = (bf16[4,208,128]{2,1,0:T(8,128)(2,1)S(1)}, bf16[4,208,128]{2,1,0:T(8,128)(2,1)S(1)}, u32[]{:S(2)}, u32[]{:S(2)}) collective-permute-start(bf16[4,208,128]{2,1,0:T(8,128)(2,1)S(1)} %get-tuple-element.52), channel_id=1, source_target_pairs={{0,16},{8,24},{16,0},{24,8},{1,17},{9,25},{17,1},{25,9},{2,18},{10... | collective-permute-start | bytes 638984 | tf_op jit(solution)/shard_map/ppermute | solution.py:59
  92.9 5.4 %collective-permute-start.21 = (bf16[208,128]{1,0:T(8,128)(2,1)S(1)}, bf16[208,128]{1,0:T(8,128)(2,1)S(1)}, u32[]{:S(2)}, u32[]{:S(2)}) collective-permute-start(bf16[208,128]{1,0:T(8,128)(2,1)S(1)} %get-tuple-element.59), channel_id=1, source_target_pairs={{0,2},{2,4},{4,6},{6,0},{1,3},{3,5},{5,7},{7,1},{8,10},{10,12},{12... | collective-permute-start | bytes 159752 | tf_op jit(solution)/shard_map/ppermute | solution.py:59
  93.5 5.0 %collective-permute-start.23 = (bf16[208,128]{1,0:T(8,128)(2,1)S(1)}, bf16[208,128]{1,0:T(8,128)(2,1)S(1)}, u32[]{:S(2)}, u32[]{:S(2)}) collective-permute-start(bf16[208,128]{1,0:T(8,128)(2,1)S(1)} %get-tuple-element.60), channel_id=1, source_target_pairs={{0,6},{2,0},{4,2},{6,4},{1,7},{3,1},{5,3},{7,5},{8,14},{10,8},{12,... | collective-permute-start | bytes 159752 | tf_op jit(solution)/shard_map/ppermute | solution.py:59
  96.2 5.6 %collective-permute-start.22 = (bf16[208,128]{1,0:T(8,128)(2,1)S(1)}, bf16[208,128]{1,0:T(8,128)(2,1)S(1)}, u32[]{:S(2)}, u32[]{:S(2)}) collective-permute-start(bf16[208,128]{1,0:T(8,128)(2,1)S(1)} %get-tuple-element.61), channel_id=1, source_target_pairs={{0,4},{2,6},{4,0},{6,2},{1,5},{3,7},{5,1},{7,3},{8,12},{10,14},{12... | collective-permute-start | bytes 159752 | tf_op jit(solution)/shard_map/ppermute | solution.py:59
  101.9 5.7 %collective-permute-start.26 = (bf16[208,128]{1,0:T(8,128)(2,1)S(1)}, bf16[208,128]{1,0:T(8,128)(2,1)S(1)}, u32[]{:S(2)}, u32[]{:S(2)}) collective-permute-start(bf16[208,128]{1,0:T(8,128)(2,1)S(1)} %add_convert_fusion.3), channel_id=1, source_target_pairs={{0,32},{32,64},{64,96},{96,0},{1,33},{33,65},{65,97},{97,1},{2,34}... | collective-permute-start | bytes 159752 | tf_op jit(solution)/shard_map/ppermute | solution.py:15
  103.5 5.6 %collective-permute-start.25 = (bf16[208,128]{1,0:T(8,128)(2,1)S(1)}, bf16[208,128]{1,0:T(8,128)(2,1)S(1)}, u32[]{:S(2)}, u32[]{:S(2)}) collective-permute-start(bf16[208,128]{1,0:T(8,128)(2,1)S(1)} %add_convert_fusion.3), channel_id=1, source_target_pairs={{0,64},{32,96},{64,0},{96,32},{1,65},{33,97},{65,1},{97,33},{2,66}... | collective-permute-start | bytes 159752 | tf_op jit(solution)/shard_map/ppermute | solution.py:15
  106.2 4.1 %collective-permute-start.24 = (bf16[208,128]{1,0:T(8,128)(2,1)S(1)}, bf16[208,128]{1,0:T(8,128)(2,1)S(1)}, u32[]{:S(2)}, u32[]{:S(2)}) collective-permute-start(bf16[208,128]{1,0:T(8,128)(2,1)S(1)} %add_convert_fusion.3), channel_id=1, source_target_pairs={{0,96},{32,0},{64,32},{96,64},{1,97},{33,1},{65,33},{97,65},{2,98}... | collective-permute-start | bytes 159752 | tf_op jit(solution)/shard_map/ppermute | solution.py:15
  111.1 114.6 %copy-start.2 = (bf16[1,208,6656]{2,1,0:T(8,128)(2,1)S(1)}, bf16[1,208,6656]{2,1,0:T(8,128)(2,1)}, u32[]{:S(2)}) copy-start(bf16[1,208,6656]{2,1,0:T(8,128)(2,1)} %param.19) | copy-start | bytes 8306692
  111.2 114.5 %all-gather.7.cloned.1.call-start = ((), (), s32[]{:S(2)}) async-start(), calls=%async_computation.1 | async-start | bytes 7028736 | tf_op jit(solution)/shard_map/all_gather | solution.py:118
  166.6 73.0 %copy-start.16 = (bf16[208,512]{1,0:T(8,128)(2,1)}, bf16[208,512]{1,0:T(8,128)(2,1)S(1)}, u32[]{:S(2)}) copy-start(bf16[208,512]{1,0:T(8,128)(2,1)S(1)} %fusion.27) | copy-start | bytes 638980
  166.6 9.3 %collective-permute-start.27 = (bf16[208,512]{1,0:T(8,128)(2,1)S(1)}, bf16[208,512]{1,0:T(8,128)(2,1)S(1)}, u32[]{:S(2)}, u32[]{:S(2)}) collective-permute-start(bf16[208,512]{1,0:T(8,128)(2,1)S(1)} %fusion.27), channel_id=1, source_target_pairs={{32,0},{64,32},{96,64},{33,1},{65,33},{97,65},{34,2},{66,34},{98,6... | collective-permute-start | bytes 638984 | tf_op jit(solution)/shard_map/ppermute | solution.py:123
  175.9 0.7 copy-start.12
  176.6 112.8 %all-gather.9.cloned.1.call-start = ((), (), s32[]{:S(2)}) async-start(), calls=%async_computation.2 | async-start | bytes 7028736 | tf_op jit(solution)/shard_map/all_gather | solution.py:118
  230.2 9.3 %copy-start.18 = (bf16[208,512]{1,0:T(8,128)(2,1)}, bf16[208,512]{1,0:T(8,128)(2,1)S(1)}, u32[]{:S(2)}) copy-start(bf16[208,512]{1,0:T(8,128)(2,1)S(1)} %add_convert_fusion.2) | copy-start | bytes 638980
  230.2 9.3 %collective-permute-start.28 = (bf16[208,512]{1,0:T(8,128)(2,1)S(1)}, bf16[208,512]{1,0:T(8,128)(2,1)S(1)}, u32[]{:S(2)}, u32[]{:S(2)}) collective-permute-start(bf16[208,512]{1,0:T(8,128)(2,1)S(1)} %add_convert_fusion.2), channel_id=1, source_target_pairs={{32,0},{64,32},{96,64},{33,1},{65,33},{97,65},{34,2},{66,34},{98,6... | collective-permute-start | bytes 638984 | tf_op jit(solution)/shard_map/ppermute | solution.py:123
  239.5 0.7 copy-start.13
  240.2 63.7 %copy-start.9 = (bf16[1,512,208]{1,2,0:T(8,128)(2,1)S(1)}, bf16[1,512,208]{1,2,0:T(8,128)(2,1)}, u32[]{:S(2)}) copy-start(bf16[1,512,208]{1,2,0:T(8,128)(2,1)} %param.18) | copy-start | bytes 638980
  240.3 112.8 %all-gather.11.cloned.1.call-start = ((), (), s32[]{:S(2)}) async-start(), calls=%async_computation.3 | async-start | bytes 7028736 | tf_op jit(solution)/shard_map/all_gather | solution.py:118
  293.9 10.0 %copy-start.20 = (bf16[208,512]{1,0:T(8,128)(2,1)}, bf16[208,512]{1,0:T(8,128)(2,1)S(1)}, u32[]{:S(2)}) copy-start(bf16[208,512]{1,0:T(8,128)(2,1)S(1)} %add_convert_fusion.1) | copy-start | bytes 638980
  293.9 9.3 %collective-permute-start.29 = (bf16[208,512]{1,0:T(8,128)(2,1)S(1)}, bf16[208,512]{1,0:T(8,128)(2,1)S(1)}, u32[]{:S(2)}, u32[]{:S(2)}) collective-permute-start(bf16[208,512]{1,0:T(8,128)(2,1)S(1)} %add_convert_fusion.1), channel_id=1, source_target_pairs={{32,0},{64,32},{96,64},{33,1},{65,33},{97,65},{34,2},{66,34},{98,6... | collective-permute-start | bytes 638984 | tf_op jit(solution)/shard_map/ppermute | solution.py:123
  303.2 0.7 copy-start.10
  360.7 3.4 copy-start.15
  360.7 4.6 %copy-start = (f32[208,6656]{1,0:T(8,128)S(1)}, f32[208,6656]{1,0:T(8,128)}, u32[]{:S(2)}) copy-start(f32[208,6656]{1,0:T(8,128)} %get-tuple-element.79) | copy-start | bytes 16613380
  360.7 6.6 %copy-start.14 = (f32[1,6656]{1,0:T(1,128)S(1)}, f32[1,6656]{1,0:T(1,128)}, u32[]{:S(2)}) copy-start(f32[1,6656]{1,0:T(1,128)} %param.21) | copy-start | bytes 79876
  360.7 27.9 %copy-start.11 = (bf16[208,512]{1,0:T(8,128)(2,1)S(1)}, bf16[208,512]{1,0:T(8,128)(2,1)}, u32[]{:S(2)}) copy-start(bf16[208,512]{1,0:T(8,128)(2,1)} %copy-done.10) | copy-start | bytes 638980
  360.7 27.9 %copy-start.17 = (bf16[208,512]{1,0:T(8,128)(2,1)S(1)}, bf16[208,512]{1,0:T(8,128)(2,1)}, u32[]{:S(2)}) copy-start(bf16[208,512]{1,0:T(8,128)(2,1)} %copy-done.16) | copy-start | bytes 638980
  360.7 27.9 %copy-start.19 = (bf16[208,512]{1,0:T(8,128)(2,1)S(1)}, bf16[208,512]{1,0:T(8,128)(2,1)}, u32[]{:S(2)}) copy-start(bf16[208,512]{1,0:T(8,128)(2,1)} %copy-done.18) | copy-start | bytes 638980
  360.7 27.8 %copy-start.21 = (bf16[208,512]{1,0:T(8,128)(2,1)S(1)}, bf16[208,512]{1,0:T(8,128)(2,1)}, u32[]{:S(2)}) copy-start(bf16[208,512]{1,0:T(8,128)(2,1)} %copy-done.20) | copy-start | bytes 638980
  367.0 1.3 collective-permute-start.30
  368.3 16.5 %collective-permute-start.32 = (f32[105,128]{1,0:T(8,128)S(1)}, f32[105,128]{1,0:T(8,128)S(1)}, u32[]{:S(2)}, u32[]{:S(2)}) collective-permute-start(f32[105,128]{1,0:T(8,128)S(1)} %fusion.45), channel_id=1, source_target_pairs={{0,6},{2,0},{4,2},{6,4},{1,7},{3,1},{5,3},{7,5},{8,14},{10,8},{12,... | collective-permute-start | bytes 161288 | tf_op jit(solution)/shard_map/ppermute | solution.py:15
  370.2 14.6 %collective-permute-start.33 = (f32[105,128]{1,0:T(8,128)S(1)}, f32[105,128]{1,0:T(8,128)S(1)}, u32[]{:S(2)}, u32[]{:S(2)}) collective-permute-start(f32[105,128]{1,0:T(8,128)S(1)} %fusion.45), channel_id=1, source_target_pairs={{0,2},{2,4},{4,6},{6,0},{1,3},{3,5},{5,7},{7,1},{8,10},{10,12},{12... | collective-permute-start | bytes 161288 | tf_op jit(solution)/shard_map/ppermute | solution.py:15
  370.4 14.5 %collective-permute-start.31 = (f32[105,128]{1,0:T(8,128)S(1)}, f32[105,128]{1,0:T(8,128)S(1)}, u32[]{:S(2)}, u32[]{:S(2)}) collective-permute-start(f32[105,128]{1,0:T(8,128)S(1)} %fusion.45), channel_id=1, source_target_pairs={{0,4},{2,6},{4,0},{6,2},{1,5},{3,7},{5,1},{7,3},{8,12},{10,14},{12... | collective-permute-start | bytes 161288 | tf_op jit(solution)/shard_map/ppermute | solution.py:15
  373.6 9.8 %collective-permute-start.16 = (f32[1]{0:T(128)}, f32[1]{0:T(128)}, u32[]{:S(2)}, u32[]{:S(2)}) collective-permute-start(f32[1]{0:T(128)} %bitcast.19), channel_id=1, source_target_pairs={{0,32},{32,64},{64,96},{96,0},{1,33},{33,65},{65,97},{97,1},{2,34}... | collective-permute-start | bytes 20 | tf_op jit(solution)/shard_map/ppermute | solution.py:15
  373.6 5.3 %collective-permute-start.14 = (f32[1]{0:T(128)}, f32[1]{0:T(128)}, u32[]{:S(2)}, u32[]{:S(2)}) collective-permute-start(f32[1]{0:T(128)} %bitcast.19), channel_id=1, source_target_pairs={{0,64},{32,96},{64,0},{96,32},{1,65},{33,97},{65,1},{97,33},{2,66}... | collective-permute-start | bytes 20 | tf_op jit(solution)/shard_map/ppermute | solution.py:15
  378.9 4.7 %collective-permute-start.15 = (f32[1]{0:T(128)}, f32[1]{0:T(128)}, u32[]{:S(2)}, u32[]{:S(2)}) collective-permute-start(f32[1]{0:T(128)} %bitcast.19), channel_id=1, source_target_pairs={{0,96},{32,0},{64,32},{96,64},{1,97},{33,1},{65,33},{97,65},{2,98}... | collective-permute-start | bytes 20 | tf_op jit(solution)/shard_map/ppermute | solution.py:15
  384.9 8.9 %collective-permute-start.36 = (f32[105,128]{1,0:T(8,128)S(1)}, f32[105,128]{1,0:T(8,128)S(1)}, u32[]{:S(2)}, u32[]{:S(2)}) collective-permute-start(f32[105,128]{1,0:T(8,128)S(1)} %add_add_fusion.1), channel_id=1, source_target_pairs={{0,8},{8,16},{16,24},{24,0},{1,9},{9,17},{17,25},{25,1},{2,10},{10... | collective-permute-start | bytes 161288 | tf_op jit(solution)/shard_map/ppermute | solution.py:15
  385.1 8.7 %collective-permute-start.35 = (f32[105,128]{1,0:T(8,128)S(1)}, f32[105,128]{1,0:T(8,128)S(1)}, u32[]{:S(2)}, u32[]{:S(2)}) collective-permute-start(f32[105,128]{1,0:T(8,128)S(1)} %add_add_fusion.1), channel_id=1, source_target_pairs={{0,24},{8,0},{16,8},{24,16},{1,25},{9,1},{17,9},{25,17},{2,26},{10... | collective-permute-start | bytes 161288 | tf_op jit(solution)/shard_map/ppermute | solution.py:15
  388.2 5.7 %collective-permute-start.34 = (f32[105,128]{1,0:T(8,128)S(1)}, f32[105,128]{1,0:T(8,128)S(1)}, u32[]{:S(2)}, u32[]{:S(2)}) collective-permute-start(f32[105,128]{1,0:T(8,128)S(1)} %add_add_fusion.1), channel_id=1, source_target_pairs={{0,16},{8,24},{16,0},{24,8},{1,17},{9,25},{17,1},{25,9},{2,18},{10... | collective-permute-start | bytes 161288 | tf_op jit(solution)/shard_map/ppermute | solution.py:15
Sparse Core Ops, SparseCore 0:
  111.3 49.8 all-gather.4
  176.7 48.9 all-gather.6
  240.4 48.9 all-gather.8
  304.0 48.9 all-gather.10
